TPU v7x, 32 devices: a whole 2x2x4 slice. The times are simulated.
32 devices in a mesh: leaf: 4 (over x, core), front: 8 (over z, y), wave: 1.
Axes of the slice: x: 2, y: 2, z: 4, core: 2. Of those that a mesh axis runs over, the one named last changes fastest.
Arguments:
- sources: float32 [8192, 128], P(('wave', 'front')), may hold values from -48 to 48
- order: int32 [8192], P('front'), may hold values from 0 to 8191, as said below
- diagonal: float32 [8192], P(('wave', 'front')), may hold values from 0.1 to 2
- coupling: float32 [8192, 4096], P(('wave', 'front'), 'leaf'), may hold values from -0.0625 to 0.0625
- interior_inverse: float32 [64, 64, 64], P(('wave', 'leaf')), may hold values from -2 to 6, as said below
- interior_load: float32 [64, 64, 128], P(('wave', 'leaf')), may hold values from -6 to 6
Outputs:
- solution: float32 [8192, 128], P(('wave', 'front'))
- interior_solution: float32 [64, 64, 128], P(('wave', 'leaf'))
Inputs may be any that keep to these rules, and one draw needn't show every extreme that they name: `order`: each aligned block of 1024 entries is a permutation of that block's own indices. `interior_inverse`: each matrix is symmetric positive definite.
All inputs are finite; a program needn't handle non-finite values.
Results may differ from a plain program's by a relative error of at most 0.0003.
Values sent between devices are 32-bit elements; how exact they have to be, the bound alone decides.
No kernel may reach another device: no remote copies, remote signals or barrier semaphores. Data moves between devices by JAX's collectives and lax.ppermute only.
A program may use at most 64 MiB of HBM per device.

v0:
```python
import jax
import jax.numpy as jnp
from jax import lax
from jax.sharding import PartitionSpec as P

ITERS = 4
HIGHEST = lax.Precision.HIGHEST


def couple(coupling, field):
    partial_sums = jnp.einsum("sk,sn->kn", coupling, field, precision=HIGHEST)
    return lax.psum(partial_sums, "front")


def condense(interior_inverse, projected):
    shaped = projected.reshape(
        interior_inverse.shape[0], interior_inverse.shape[1], projected.shape[1]
    )
    return jnp.einsum("bij,bjn->bin", interior_inverse, shaped, precision=HIGHEST)


def cg_update(solution, residual, direction, image, norm_now, own):
    mine_dir = own(direction)
    mine_res = own(residual)
    mine_img = own(image)
    curvature, cross, square = lax.psum(
        (
            jnp.sum(mine_dir * mine_img, axis=0),
            jnp.sum(mine_res * mine_img, axis=0),
            jnp.sum(mine_img * mine_img, axis=0),
        ),
        ("leaf", "front"),
    )
    step_size = norm_now / curvature
    norm_next = norm_now - 2.0 * step_size * cross + step_size * step_size * square
    solution = solution + step_size * direction
    residual = residual - step_size * image
    direction = residual + norm_next / norm_now * direction
    return (solution, residual, direction, norm_next)


def per_device(sources, order, diagonal, coupling, interior_inverse, interior_load):
    rows_here = sources.shape[0]
    columns = sources.shape[1]
    positions = order - lax.axis_index("front") * rows_here
    loads = jnp.take(sources, positions, axis=0)
    share_rows = rows_here // lax.axis_size("leaf")
    first_row = lax.axis_index("leaf") * share_rows

    def own_rows(field):
        return lax.dynamic_slice_in_dim(field, first_row, share_rows, 0)

    start_share = own_rows(loads)
    start_total = lax.psum(jnp.sum(start_share * start_share, axis=0), ("leaf", "front"))
    solution = jnp.zeros_like(loads)
    residual = loads
    direction = loads
    norm_now = start_total
    for iteration in range(ITERS):
        coeffs = condense(interior_inverse, couple(coupling, direction)).reshape(-1, columns)
        spread_term = jnp.einsum("sk,kn->sn", coupling, coeffs, precision=HIGHEST)
        image = diagonal[:, None] * direction + lax.psum(spread_term, "leaf")
        solution, residual, direction, norm_now = cg_update(
            solution, residual, direction, image, norm_now, own_rows
        )
    projected = couple(coupling, solution).reshape(interior_load.shape)
    interior_solution = jnp.einsum(
        "bij,bjn->bin", interior_inverse, interior_load - projected, precision=HIGHEST
    )
    return (solution, interior_solution)


def solution(mesh):
    return jax.shard_map(
        per_device,
        mesh=mesh,
        in_specs=(
            P(("wave", "front"), None),
            P("front"),
            P(("wave", "front")),
            P(("wave", "front"), "leaf"),
            P(("wave", "leaf"), None, None),
            P(("wave", "leaf"), None, None),
        ),
        out_specs=(P(("wave", "front"), None), P(("wave", "leaf"), None, None)),
        check_vma=False,
    )
```

profile of v0, /device:TPU:0, one launch (start us, length us, event | category | flops | bytes accessed | tf_op | source)
XLA Modules:
  0.0 752.2 jit_solution(4193403296460094578)
XLA Ops:
  8.7 3.8 gather_fusion
  12.8 4.6 convolution_bitcast_fusion.9
  18.4 75.6 %all-reduce.13.cloned.1.call-done = f32[16,64,128]{2,1,0:T(8,128)} async-done(((f32[16,64,128]{2,1,0:T(8,128)}), f32[16,64,128]{2,1,0:T(8,128)}) %all-reduce.13.cloned.1.call-update) | async-done | bytes 524304 | tf_op jit(solution)/shard_map/psum | solution.py:12
  94.0 1.7 fusion.7
  95.7 7.5 %convolution_bitcast_fusion.8 = f32[1024,128]{0,1:T(8,128)} fusion(f32[1024,128]{1,0:T(8,128)S(1)} %bitcast.64, f32[1024,1024]{1,0:T(8,128)} %param.9), kind=kOutput, calls=%fused_computation.9 | convolution fusion | flops 1610612736 | bytes 5242880 | tf_op jit(solution)/shard_map/sk,kn->sn/dot_general | solution.py:61
  103.3 32.7 %all-reduce.15.cloned.1.call-done = f32[1024,128]{0,1:T(8,128)} async-done(((f32[1024,128]{0,1:T(8,128)}), f32[1024,128]{0,1:T(8,128)}) %all-reduce.15.cloned.1.call-update) | async-done | bytes 524304 | tf_op jit(solution)/shard_map/psum | solution.py:62
  136.0 1.1 multiply_add_fusion.6
  137.3 39.5 %all-reduce.2 = (f32[128]{0:T(128)S(1)}, f32[128]{0:T(128)S(1)}, f32[128]{0:T(128)S(1)}) all-reduce(f32[128]{0:T(128)S(1)} %get-tuple-element.14, f32[128]{0:T(128)S(1)} %get-tuple-element.13, f32[128]{0:T(128)S(1)} %get-tuple-element.12), channel_id=1, replica_groups=mesh['leaf'=4,'front'=8,'wave'=1] {'leaf','front'}, use_global_device_ids=true, to_apply=%region_1.2 | all-reduce | flops 384 | bytes 3072 | tf_op jit(solution)/shard_map/psum | solution.py:54
  176.9 4.6 convolution_bitcast_fusion.7
  182.8 73.2 %all-reduce.17.cloned.1.call-done = f32[16,64,128]{2,1,0:T(8,128)} async-done(((f32[16,64,128]{2,1,0:T(8,128)}), f32[16,64,128]{2,1,0:T(8,128)}) %all-reduce.17.cloned.1.call-update) | async-done | bytes 524304 | tf_op jit(solution)/shard_map/psum | solution.py:12
  255.9 1.7 fusion.8
  257.6 7.5 convolution_bitcast_fusion.6
  265.1 32.7 %all-reduce.19.cloned.1.call-done = f32[1024,128]{0,1:T(8,128)} async-done(((f32[1024,128]{0,1:T(8,128)}), f32[1024,128]{0,1:T(8,128)}) %all-reduce.19.cloned.1.call-update) | async-done | bytes 524304 | tf_op jit(solution)/shard_map/psum | solution.py:62
  297.8 1.1 multiply_add_fusion.4
  299.1 39.5 %all-reduce.1 = (f32[128]{0:T(128)S(1)}, f32[128]{0:T(128)S(1)}, f32[128]{0:T(128)S(1)}) all-reduce(f32[128]{0:T(128)S(1)} %get-tuple-element.11, f32[128]{0:T(128)S(1)} %get-tuple-element.10, f32[128]{0:T(128)S(1)} %get-tuple-element.9), channel_id=1, replica_groups=mesh['leaf'=4,'front'=8,'wave'=1] {'leaf','front'}, use_global_device_ids=true, to_apply=%region_11.12 | all-reduce | flops 384 | bytes 3072 | tf_op jit(solution)/shard_map/psum | solution.py:26
  339.5 4.6 convolution_bitcast_fusion.5
  345.4 73.1 %all-reduce.21.cloned.1.call-done = f32[16,64,128]{2,1,0:T(8,128)} async-done(((f32[16,64,128]{2,1,0:T(8,128)}), f32[16,64,128]{2,1,0:T(8,128)}) %all-reduce.21.cloned.1.call-update) | async-done | bytes 524304 | tf_op jit(solution)/shard_map/psum | solution.py:12
  418.5 1.7 fusion.9
  420.2 7.5 convolution_bitcast_fusion.4
  427.7 32.7 %all-reduce.23.cloned.1.call-done = f32[1024,128]{0,1:T(8,128)} async-done(((f32[1024,128]{0,1:T(8,128)}), f32[1024,128]{0,1:T(8,128)}) %all-reduce.23.cloned.1.call-update) | async-done | bytes 524304 | tf_op jit(solution)/shard_map/psum | solution.py:62
  460.4 1.1 multiply_add_fusion.2
  461.7 39.5 %all-reduce = (f32[128]{0:T(128)S(1)}, f32[128]{0:T(128)S(1)}, f32[128]{0:T(128)S(1)}) all-reduce(f32[128]{0:T(128)S(1)} %get-tuple-element.7, f32[128]{0:T(128)S(1)} %get-tuple-element.8, f32[128]{0:T(128)S(1)} %get-tuple-element.6), channel_id=1, replica_groups=mesh['leaf'=4,'front'=8,'wave'=1] {'leaf','front'}, use_global_device_ids=true, to_apply=%region_23.24 | all-reduce | flops 384 | bytes 3072 | tf_op jit(solution)/shard_map/psum | solution.py:26
  501.2 1.2 multiply_add_fusion.1
  502.4 4.6 convolution_bitcast_fusion.3
  508.4 73.1 %all-reduce.25.cloned.1.call-done = f32[16,64,128]{2,1,0:T(8,128)} async-done(((f32[16,64,128]{2,1,0:T(8,128)}), f32[16,64,128]{2,1,0:T(8,128)}) %all-reduce.25.cloned.1.call-update) | async-done | bytes 524304 | tf_op jit(solution)/shard_map/psum | solution.py:12
  581.4 1.7 fusion.10
  583.1 7.5 %convolution_bitcast_fusion.2 = f32[1024,128]{0,1:T(8,128)} fusion(f32[1024,128]{1,0:T(8,128)S(1)} %bitcast.67, f32[1024,1024]{1,0:T(8,128)} %param.9), kind=kOutput, calls=%fused_computation.3 | convolution fusion | flops 1610612736 | bytes 5242880 | tf_op jit(solution)/shard_map/sk,kn->sn/dot_general | solution.py:61
  590.8 32.6 %all-reduce.27.cloned.1.call-done = f32[1024,128]{0,1:T(8,128)} async-done(((f32[1024,128]{0,1:T(8,128)}), f32[1024,128]{0,1:T(8,128)}) %all-reduce.27.cloned.1.call-update) | async-done | bytes 524304 | tf_op jit(solution)/shard_map/psum | solution.py:62
  624.4 39.4 %psum.153 = f32[128]{0:T(128)S(1)} all-reduce(f32[128]{0:T(128)S(1)} %fusion.2), channel_id=1, replica_groups=mesh['leaf'=4,'front'=8,'wave'=1] {'leaf','front'}, use_global_device_ids=true, to_apply=%region_27.28 | all-reduce | flops 128 | bytes 1024 | tf_op jit(solution)/shard_map/psum | solution.py:26
  664.1 4.6 convolution_bitcast_fusion.1
  670.8 72.4 %all-reduce.29.cloned.1.call-done = f32[16,64,128]{2,1,0:T(8,128)} async-done(((f32[16,64,128]{2,1,0:T(8,128)}), f32[16,64,128]{2,1,0:T(8,128)}) %all-reduce.29.cloned.1.call-update) | async-done | bytes 524304 | tf_op jit(solution)/shard_map/psum | solution.py:12
  743.2 2.5 convolution_bitcast_fusion
  (48 shorter events, 11.8 us)
Async XLA Ops:
  7.2 86.8 %copy-start = (f32[16,64,64]{2,1,0:T(8,128)S(1)}, f32[16,64,64]{2,1,0:T(8,128)}, u32[]{:S(2)}) copy-start(f32[16,64,64]{2,1,0:T(8,128)} %param.10) | copy-start | bytes 786436
  7.2 86.8 %all-reduce.13.cloned.1.call-start = ((), (), s32[]{:S(2)}) async-start(), calls=%async_computation | async-start | bytes 1048576 | tf_op jit(solution)/shard_map/psum | solution.py:12
  18.4 117.6 %copy-start.3 = (f32[1024]{0:T(1024)S(1)}, f32[1024]{0:T(1024)}, u32[]{:S(2)}) copy-start(f32[1024]{0:T(1024)} %param.8) | copy-start | bytes 12292
  18.4 117.6 %all-reduce.15.cloned.1.call-start = ((), (), s32[]{:S(2)}) async-start(), calls=%async_computation.1 | async-start | bytes 1048576 | tf_op jit(solution)/shard_map/psum | solution.py:62
  103.2 152.7 %all-reduce.17.cloned.1.call-start = ((), (), s32[]{:S(2)}) async-start(), calls=%async_computation.2 | async-start | bytes 1048576 | tf_op jit(solution)/shard_map/psum | solution.py:12
  182.5 115.3 %all-reduce.19.cloned.1.call-start = ((), (), s32[]{:S(2)}) async-start(), calls=%async_computation.3 | async-start | bytes 1048576 | tf_op jit(solution)/shard_map/psum | solution.py:62
  265.1 153.5 %all-reduce.21.cloned.1.call-start = ((), (), s32[]{:S(2)}) async-start(), calls=%async_computation.4 | async-start | bytes 1048576 | tf_op jit(solution)/shard_map/psum | solution.py:12
  345.1 116.4 %copy-start.1 = (f32[1024,128]{0,1:T(8,128)S(1)}, f32[1024,128]{0,1:T(8,128)}, u32[]{:S(2)}) copy-start(f32[1024,128]{0,1:T(8,128)} %get-tuple-element.28) | copy-start | bytes 1572868
  345.1 115.3 %all-reduce.23.cloned.1.call-start = ((), (), s32[]{:S(2)}) async-start(), calls=%async_computation.5 | async-start | bytes 1048576 | tf_op jit(solution)/shard_map/psum | solution.py:62
  427.7 153.7 %all-reduce.25.cloned.1.call-start = ((), (), s32[]{:S(2)}) async-start(), calls=%async_computation.6 | async-start | bytes 1048576 | tf_op jit(solution)/shard_map/psum | solution.py:12
  508.0 115.4 %all-reduce.27.cloned.1.call-start = ((), (), s32[]{:S(2)}) async-start(), calls=%async_computation.7 | async-start | bytes 1048576 | tf_op jit(solution)/shard_map/psum | solution.py:62
  590.7 152.5 %all-reduce.29.cloned.1.call-start = ((), (), s32[]{:S(2)}) async-start(), calls=%async_computation.8 | async-start | bytes 1048576 | tf_op jit(solution)/shard_map/psum | solution.py:12
  664.1 79.1 %copy-start.2 = (f32[16,64,128]{2,1,0:T(8,128)S(1)}, f32[16,64,128]{2,1,0:T(8,128)}, u32[]{:S(2)}) copy-start(f32[16,64,128]{2,1,0:T(8,128)} %param.11) | copy-start | bytes 1572868
Sparse Core Ops, SparseCore 0:
  18.5 75.4 all-reduce.12
  103.3 32.5 all-reduce.14
  182.6 73.2 all-reduce.16
  265.2 32.5 all-reduce.18
  345.3 73.2 all-reduce.20
  427.8 32.5 all-reduce.22
  508.2 73.2 all-reduce.24
  590.8 32.5 all-reduce.26
  669.9 73.2 all-reduce.28
where the time goes:
time: 753 us; the launch traced here: 752 us
  waiting for transfers between devices  498 us (66%)
  blocking collectives  158 us (21%)
  matrix products  62.1 us (8%)
  between operations  14 us (2%)
  local copies, waits for them, and re-layouts  10.1 us (1%)
  other arithmetic  8.92 us (1%)
    psum x5, waiting for transfers between devices, couple(): return lax.psum(partial_sums, 'front')  367 us
    psum x4, waiting for transfers between devices, per_device(): image = diagonal[:, None] * direction + lax.psum(spread_term, 'leaf')  131 us
    psum x3, blocking collectives, cg_update(): lax.psum((jnp.sum(mine_dir * mine_img, axis=0), jnp.sum(mine_res * mine_i...  118 us
    psum x1, blocking collectives, per_device(): lax.psum(jnp.sum(start_share * start_share, axis=0), ('leaf', 'front'))  39.5 us
    dot_general x4, matrix products, per_device(): spread_term = jnp.einsum('sk,kn->sn', coupling, coeffs, precision=HIGHEST)  30 us
    dot_general x5, matrix products, couple(): partial_sums = jnp.einsum('sk,sn->kn', coupling, field, precision=HIGHEST)  23 us
  transfers between devices with their start and end apart: 9, of which 9 were waited for; matrix products, arithmetic and copies ran while one was open for 0% of the time, Pallas kernels for 0%

commit v1 on v0

--- a/solution.py
+++ b/solution.py
@@ -59,7 +59,7 @@
     for iteration in range(ITERS):
         coeffs = condense(interior_inverse, couple(coupling, direction)).reshape(-1, columns)
         spread_term = jnp.einsum("sk,kn->sn", coupling, coeffs, precision=HIGHEST)
-        image = diagonal[:, None] * direction + lax.psum(spread_term, "leaf")
+        image = diagonal[:, None] * direction + jnp.sum(lax.all_gather(spread_term, "leaf"), axis=0)
         solution, residual, direction, norm_now = cg_update(
             solution, residual, direction, image, norm_now, own_rows
         )

time: 753 us -> 744 us (0.988); the launches traced: 752 us -> 736 us
  waiting for transfers between devices: 498 us -> 457 us
  local copies, waits for them, and re-layouts: 10.1 us -> 25 us
  other arithmetic: 8.92 us -> 17.9 us
    psum x4 -> x0, waiting for transfers between devices: 131 us -> none  [per_device(): image = diagonal[:, None] * direction + lax.psum(spread_term, 'leaf')]
    all_gather x0 -> x4, waiting for transfers between devices: none -> 87.3 us  [per_device(): lax.all_gather(spread_term, 'leaf')]
    all_gather x0 -> x4, local copies, waits for them, and re-layouts: none -> 13.6 us  [per_device(): lax.all_gather(spread_term, 'leaf')]
    reduce_sum x0 -> x4, other arithmetic: none -> 10.8 us  [per_device(): jnp.sum(lax.all_gather(spread_term, 'leaf'), axis=0)]
where the time goes in v1:
time: 744 us; the launch traced here: 736 us
  waiting for transfers between devices  457 us (61%)
  blocking collectives  159 us (21%)
  matrix products  62.4 us (8%)
  local copies, waits for them, and re-layouts  25 us (3%)
  other arithmetic  17.9 us (2%)
  between operations  14.4 us (2%)
    psum x5, waiting for transfers between devices, couple(): return lax.psum(partial_sums, 'front')  370 us
    psum x3, blocking collectives, cg_update(): lax.psum((jnp.sum(mine_dir * mine_img, axis=0), jnp.sum(mine_res * mine_i...  119 us
    all_gather x4, waiting for transfers between devices, per_device(): lax.all_gather(spread_term, 'leaf')  87.3 us
    psum x1, blocking collectives, per_device(): lax.psum(jnp.sum(start_share * start_share, axis=0), ('leaf', 'front'))  39.9 us
    dot_general x4, matrix products, per_device(): spread_term = jnp.einsum('sk,kn->sn', coupling, coeffs, precision=HIGHEST)  30.1 us
    dot_general x5, matrix products, couple(): partial_sums = jnp.einsum('sk,sn->kn', coupling, field, precision=HIGHEST)  23.2 us
  transfers between devices with their start and end apart: 9, of which 9 were waited for; matrix products, arithmetic and copies ran while one was open for 0% of the time, Pallas kernels for 0%

profile of v1, /device:TPU:0, one launch (start us, length us, event | category | flops | bytes accessed | tf_op | source)
XLA Modules:
  0.0 735.6 jit_solution(1935537549307374871)
XLA Ops:
  8.7 3.8 gather_fusion
  13.5 4.7 convolution_bitcast_fusion.9
  19.3 75.6 %all-reduce.9.cloned.1.call-done = f32[16,64,128]{2,1,0:T(8,128)} async-done(((f32[16,64,128]{2,1,0:T(8,128)}), f32[16,64,128]{2,1,0:T(8,128)}) %all-reduce.9.cloned.1.call-update) | async-done | bytes 524304 | tf_op jit(solution)/shard_map/psum | solution.py:12
  96.5 7.6 %convolution_bitcast_fusion.8 = f32[1024,128]{0,1:T(8,128)} fusion(f32[1024,128]{1,0:T(8,128)S(1)} %bitcast.72, f32[1024,1024]{1,0:T(8,128)} %param.9), kind=kOutput, calls=%fused_computation.9 | convolution fusion | flops 1610612736 | bytes 5242880 | tf_op jit(solution)/shard_map/sk,kn->sn/dot_general | solution.py:61
  104.1 21.8 %all-gather.9.cloned.1.call-done = f32[4096,128]{0,1:T(8,128)} async-done(((f32[1024,128]{0,1:T(8,128)}), f32[4096,128]{0,1:T(8,128)}) %all-gather.9.cloned.1.call-update) | async-done | bytes 2097168 | tf_op jit(solution)/shard_map/all_gather | solution.py:62
  126.0 2.7 reshape.61
  128.7 2.2 reduce_sum.131
  133.4 39.9 %all-reduce.2 = (f32[128]{0:T(128)S(1)}, f32[128]{0:T(128)S(1)}, f32[128]{0:T(128)S(1)}) all-reduce(f32[128]{0:T(128)S(1)} %get-tuple-element.10, f32[128]{0:T(128)S(1)} %get-tuple-element.9, f32[128]{0:T(128)S(1)} %get-tuple-element.8), channel_id=1, replica_groups=mesh['leaf'=4,'front'=8,'wave'=1] {'leaf','front'}, use_global_device_ids=true, to_apply=%region_1.2 | all-reduce | flops 384 | bytes 3072 | tf_op jit(solution)/shard_map/psum | solution.py:54
  173.5 4.6 convolution_bitcast_fusion.7
  179.2 73.5 %all-reduce.11.cloned.1.call-done = f32[16,64,128]{2,1,0:T(8,128)} async-done(((f32[16,64,128]{2,1,0:T(8,128)}), f32[16,64,128]{2,1,0:T(8,128)}) %all-reduce.11.cloned.1.call-update) | async-done | bytes 524304 | tf_op jit(solution)/shard_map/psum | solution.py:12
  254.3 7.5 %convolution_bitcast_fusion.6 = f32[1024,128]{0,1:T(8,128)} fusion(f32[1024,128]{1,0:T(8,128)S(1)} %bitcast.73, f32[1024,1024]{1,0:T(8,128)} %param.9), kind=kOutput, calls=%fused_computation.7 | convolution fusion | flops 1610612736 | bytes 5242880 | tf_op jit(solution)/shard_map/sk,kn->sn/dot_general | solution.py:61
  261.9 21.8 %all-gather.11.cloned.1.call-done = f32[4096,128]{0,1:T(8,128)} async-done(((f32[1024,128]{0,1:T(8,128)}), f32[4096,128]{0,1:T(8,128)}) %all-gather.11.cloned.1.call-update) | async-done | bytes 2097168 | tf_op jit(solution)/shard_map/all_gather | solution.py:62
  283.7 3.6 reshape.62
  287.3 2.9 reduce_sum.134
  290.7 39.5 %all-reduce.1 = (f32[128]{0:T(128)S(1)}, f32[128]{0:T(128)S(1)}, f32[128]{0:T(128)S(1)}) all-reduce(f32[128]{0:T(128)S(1)} %get-tuple-element.7, f32[128]{0:T(128)S(1)} %get-tuple-element.6, f32[128]{0:T(128)S(1)} %get-tuple-element.5), channel_id=1, replica_groups=mesh['leaf'=4,'front'=8,'wave'=1] {'leaf','front'}, use_global_device_ids=true, to_apply=%region_11.12 | all-reduce | flops 384 | bytes 3072 | tf_op jit(solution)/shard_map/psum | solution.py:26
  331.1 4.6 convolution_bitcast_fusion.5
  336.8 73.5 %all-reduce.13.cloned.1.call-done = f32[16,64,128]{2,1,0:T(8,128)} async-done(((f32[16,64,128]{2,1,0:T(8,128)}), f32[16,64,128]{2,1,0:T(8,128)}) %all-reduce.13.cloned.1.call-update) | async-done | bytes 524304 | tf_op jit(solution)/shard_map/psum | solution.py:12
  411.9 7.5 %convolution_bitcast_fusion.4 = f32[1024,128]{0,1:T(8,128)} fusion(f32[1024,128]{1,0:T(8,128)S(1)} %bitcast.74, f32[1024,1024]{1,0:T(8,128)} %param.9), kind=kOutput, calls=%fused_computation.5 | convolution fusion | flops 1610612736 | bytes 5242880 | tf_op jit(solution)/shard_map/sk,kn->sn/dot_general | solution.py:61
  419.5 21.8 %all-gather.13.cloned.1.call-done = f32[4096,128]{0,1:T(8,128)} async-done(((f32[1024,128]{0,1:T(8,128)}), f32[4096,128]{0,1:T(8,128)}) %all-gather.13.cloned.1.call-update) | async-done | bytes 2097168 | tf_op jit(solution)/shard_map/all_gather | solution.py:62
  441.4 3.6 reshape.63
  445.0 2.9 reduce_sum.138
  449.3 39.6 %all-reduce = (f32[128]{0:T(128)S(1)}, f32[128]{0:T(128)S(1)}, f32[128]{0:T(128)S(1)}) all-reduce(f32[128]{0:T(128)S(1)} %get-tuple-element.3, f32[128]{0:T(128)S(1)} %get-tuple-element.4, f32[128]{0:T(128)S(1)} %get-tuple-element.2), channel_id=1, replica_groups=mesh['leaf'=4,'front'=8,'wave'=1] {'leaf','front'}, use_global_device_ids=true, to_apply=%region_23.24 | all-reduce | flops 384 | bytes 3072 | tf_op jit(solution)/shard_map/psum | solution.py:26
  490.1 4.6 convolution_bitcast_fusion.3
  495.7 73.5 %all-reduce.15.cloned.1.call-done = f32[16,64,128]{2,1,0:T(8,128)} async-done(((f32[16,64,128]{2,1,0:T(8,128)}), f32[16,64,128]{2,1,0:T(8,128)}) %all-reduce.15.cloned.1.call-update) | async-done | bytes 524304 | tf_op jit(solution)/shard_map/psum | solution.py:12
  570.9 7.5 %convolution_bitcast_fusion.2 = f32[1024,128]{0,1:T(8,128)} fusion(f32[1024,128]{1,0:T(8,128)S(1)} %bitcast.75, f32[1024,1024]{1,0:T(8,128)} %param.9), kind=kOutput, calls=%fused_computation.3 | convolution fusion | flops 1610612736 | bytes 5242880 | tf_op jit(solution)/shard_map/sk,kn->sn/dot_general | solution.py:61
  578.6 21.8 %all-gather.15.cloned.1.call-done = f32[4096,128]{0,1:T(8,128)} async-done(((f32[1024,128]{0,1:T(8,128)}), f32[4096,128]{0,1:T(8,128)}) %all-gather.15.cloned.1.call-update) | async-done | bytes 2097168 | tf_op jit(solution)/shard_map/all_gather | solution.py:62
  600.4 3.6 reshape.64
  604.0 2.9 reduce_sum.142
  607.1 39.6 %psum.121 = f32[128]{0:T(128)S(1)} all-reduce(f32[128]{0:T(128)S(1)} %multiply_reduce_fusion), channel_id=1, replica_groups=mesh['leaf'=4,'front'=8,'wave'=1] {'leaf','front'}, use_global_device_ids=true, to_apply=%region_27.28 | all-reduce | flops 128 | bytes 1024 | tf_op jit(solution)/shard_map/psum | solution.py:26
  646.9 4.8 convolution_bitcast_fusion.1
  652.8 73.6 %all-reduce.17.cloned.1.call-done = f32[16,64,128]{2,1,0:T(8,128)} async-done(((f32[16,64,128]{2,1,0:T(8,128)}), f32[16,64,128]{2,1,0:T(8,128)}) %all-reduce.17.cloned.1.call-update) | async-done | bytes 524304 | tf_op jit(solution)/shard_map/psum | solution.py:12
  726.3 2.5 convolution_bitcast_fusion
  (61 shorter events, 21.8 us)
Async XLA Ops:
  7.2 87.7 %copy-start = (f32[16,64,64]{2,1,0:T(8,128)S(1)}, f32[16,64,64]{2,1,0:T(8,128)}, u32[]{:S(2)}) copy-start(f32[16,64,64]{2,1,0:T(8,128)} %param.10) | copy-start | bytes 786436
  7.2 87.7 %all-reduce.9.cloned.1.call-start = ((), (), s32[]{:S(2)}) async-start(), calls=%async_computation | async-start | bytes 1048576 | tf_op jit(solution)/shard_map/psum | solution.py:12
  12.7 0.8 copy-start.1
  19.2 106.7 %all-gather.9.cloned.1.call-start = ((), (), s32[]{:S(2)}) async-start(), calls=%async_computation.5 | async-start | bytes 2621440 | tf_op jit(solution)/shard_map/all_gather | solution.py:62
  104.1 28.0 %copy-start.4 = (f32[1024]{0:T(1024)S(1)}, f32[1024]{0:T(1024)}, u32[]{:S(2)}) copy-start(f32[1024]{0:T(1024)} %param.8) | copy-start | bytes 12292
  104.1 148.6 %all-reduce.11.cloned.1.call-start = ((), (), s32[]{:S(2)}) async-start(), calls=%async_computation.1 | async-start | bytes 1048576 | tf_op jit(solution)/shard_map/psum | solution.py:12
  179.1 104.6 %all-gather.11.cloned.1.call-start = ((), (), s32[]{:S(2)}) async-start(), calls=%async_computation.6 | async-start | bytes 2621440 | tf_op jit(solution)/shard_map/all_gather | solution.py:62
  261.8 148.4 %all-reduce.13.cloned.1.call-start = ((), (), s32[]{:S(2)}) async-start(), calls=%async_computation.2 | async-start | bytes 1048576 | tf_op jit(solution)/shard_map/psum | solution.py:12
  336.7 104.7 %all-gather.13.cloned.1.call-start = ((), (), s32[]{:S(2)}) async-start(), calls=%async_computation.7 | async-start | bytes 2621440 | tf_op jit(solution)/shard_map/all_gather | solution.py:62
  419.5 149.8 %all-reduce.15.cloned.1.call-start = ((), (), s32[]{:S(2)}) async-start(), calls=%async_computation.3 | async-start | bytes 1048576 | tf_op jit(solution)/shard_map/psum | solution.py:12
  495.7 104.7 %all-gather.15.cloned.1.call-start = ((), (), s32[]{:S(2)}) async-start(), calls=%async_computation.8 | async-start | bytes 2621440 | tf_op jit(solution)/shard_map/all_gather | solution.py:62
  578.5 147.9 %all-reduce.17.cloned.1.call-start = ((), (), s32[]{:S(2)}) async-start(), calls=%async_computation.4 | async-start | bytes 1048576 | tf_op jit(solution)/shard_map/psum | solution.py:12
  646.9 81.9 %copy-start.2 = (f32[1024,128]{1,0:T(8,128)}, f32[1024,128]{1,0:T(8,128)S(1)}, u32[]{:S(2)}) copy-start(f32[1024,128]{1,0:T(8,128)S(1)} %multiply_add_fusion) | copy-start | bytes 1572868
  646.9 79.4 %copy-start.3 = (f32[16,64,128]{2,1,0:T(8,128)S(1)}, f32[16,64,128]{2,1,0:T(8,128)}, u32[]{:S(2)}) copy-start(f32[16,64,128]{2,1,0:T(8,128)} %param.11) | copy-start | bytes 1572868
Sparse Core Ops, SparseCore 0:
  19.4 75.4 all-reduce.8
  104.2 21.7 all-gather.8
  179.2 73.3 all-reduce.10
  261.9 21.7 all-gather.10
  336.8 73.3 all-reduce.12
  419.6 21.7 all-gather.12
  495.8 73.3 all-reduce.14
  578.6 21.7 all-gather.14
  652.9 73.4 all-reduce.16
